TPU v7x, 32 devices: a whole 2x2x4 slice. The times are simulated.
32 devices in a mesh: shard: 2 (over y), tensor: 4 (over z), section: 4 (over x, core).
Axes of the slice: x: 2, y: 2, z: 4, core: 2. Of those that a mesh axis runs over, the one named last changes fastest.
Arguments:
- xin: bfloat16 [4, 16384, 768], P(None, ('shard', 'tensor', 'section')), may hold values from -6 to 6
- dout: bfloat16 [4, 16384, 768], P(None, ('shard', 'tensor', 'section')), may hold values from -6 to 6
- weights: bfloat16 [4, 768, 768], P(None, ('tensor', 'section')), may hold values from -0.21875 to 0.21875
- slot_block: int32 [8], replicated, may hold values from -1 to 3, as said below
- left_stat: float32 [8, 768, 768], P('shard', ('tensor', 'section')), may hold values from -1 to 10, as said below
- right_stat: float32 [8, 768, 768], P('shard', ('tensor', 'section')), may hold values from -1 to 10, as said below
- left_root: float32 [8, 768, 768], P('shard', ('tensor', 'section')), may hold values from -1 to 10, as said below
- right_root: float32 [8, 768, 768], P('shard', ('tensor', 'section')), may hold values from -1 to 10, as said below
- first_moment: float32 [8, 768, 768], P('shard', ('tensor', 'section')), may hold values from -0.3 to 0.3
- second_moment: float32 [8, 768, 768], P('shard', ('tensor', 'section')), may hold values from 0.001 to 0.01
Outputs:
- new_weights: bfloat16 [4, 768, 768], P(None, ('tensor', 'section'))
- new_left: float32 [8, 768, 768], P('shard', ('tensor', 'section'))
- new_right: float32 [8, 768, 768], P('shard', ('tensor', 'section'))
- new_first: float32 [8, 768, 768], P('shard', ('tensor', 'section'))
- new_second: float32 [8, 768, 768], P('shard', ('tensor', 'section'))
Inputs may be any that keep to these rules, and one draw needn't show every extreme that they name: `slot_block`: every block 0 to 3 stands in exactly one slot; slots 4 s to 4 s + 3 belong to shard index s; some shard index holds two blocks and none holds more; the other slots hold -1. `left_stat`: each slot is a symmetric positive definite matrix. `right_stat`: each slot is a symmetric positive definite matrix. `left_root`: each slot is a symmetric positive definite matrix. `right_root`: each slot is a symmetric positive definite matrix.
All inputs are finite; a program needn't handle non-finite values.
Results may differ from a plain program's by a relative error of at most 0.00045.
Values may be sent and summed in bfloat16 or wider, within the bound.
No kernel may reach another device: no remote copies, remote signals or barrier semaphores. Data moves between devices by JAX's collectives and lax.ppermute only.
A program may use at most 128 MiB of HBM per device.

v0:
```python
import math
import jax
import jax.numpy as jnp
from jax import lax
from jax.sharding import PartitionSpec as P


def spread(value, axis, source):
    kept = jnp.where(lax.axis_index(axis) == source, value, 0).astype(value.dtype)
    return lax.psum(kept, axis)


def absorb_slot(mine_rows, root_rows, portion, col_first):
    highest = lax.Precision.HIGHEST
    row_count = mine_rows.shape[0]
    block_part = jnp.dot(mine_rows, portion.T, precision=highest)
    own_cols = lax.dynamic_slice_in_dim(portion, col_first, row_count, 1)
    right_gram = jnp.dot(own_cols.T, portion, precision=highest)
    left_prod = jnp.dot(root_rows, portion, precision=highest)
    return (block_part, right_gram, left_prod)


def apply_slot(prod_rows, portion):
    return jnp.dot(prod_rows, portion, precision=lax.Precision.HIGHEST)


def on_device(
    xin,
    dout,
    weights,
    slot_block,
    left_stat,
    right_stat,
    left_root,
    right_root,
    first_moment,
    second_moment,
):
    block_count, tok_count, block_size = xin.shape
    slot_count, row_count = (left_stat.shape[0], left_stat.shape[1])
    group_count = lax.axis_size(("tensor", "section"))
    shard_count = lax.axis_size("shard")
    factor = 1.0 / math.sqrt(tok_count * shard_count * group_count * block_size)
    pieces_out = []
    for grad_member in range(block_count):
        cols = xin[grad_member]
        pieces_out.append(
            jnp.einsum("tr,tc->rc", cols, dout[grad_member], preferred_element_type=jnp.float32)
        )
    partial_rows = lax.psum_scatter(
        jnp.concatenate(pieces_out, axis=1) * factor,
        ("tensor", "section"),
        scatter_dimension=0,
        tiled=True,
    )
    grad_rows = lax.psum(partial_rows, "shard")
    shard_idx = lax.axis_index("shard")
    group_idx = lax.axis_index(("tensor", "section"))
    my_slots = lax.dynamic_slice_in_dim(slot_block, shard_idx * slot_count, slot_count)
    valid = my_slots >= 0
    picks = jnp.maximum(my_slots, 0)
    grad_three = grad_rows.reshape(row_count, block_count, block_size)
    mine = jnp.moveaxis(jnp.take(grad_three, picks, axis=1), 1, 0)
    col_first = group_idx * row_count
    zeros_rows = jnp.zeros((slot_count, row_count, block_size), jnp.float32)
    totals = (zeros_rows, zeros_rows, zeros_rows)
    portion = lax.all_gather(mine, ("tensor", "section"), axis=1, tiled=True)
    lefts = []
    rights = []
    prods = []
    for slot_pos in range(slot_count):
        current = (totals[0][slot_pos], totals[1][slot_pos], totals[2][slot_pos])
        result = lax.cond(
            valid[slot_pos],
            lambda values: absorb_slot(
                mine[slot_pos], left_root[slot_pos], portion[slot_pos], col_first
            ),
            lambda values: values,
            current,
        )
        lefts.append(result[0])
        rights.append(result[1])
        prods.append(result[2])
    left_gram = jnp.stack(lefts)
    right_gram = jnp.stack(rights)
    left_prod = jnp.stack(prods)
    apply_portion = lax.all_gather(right_root, ("tensor", "section"), axis=1, tiled=True)
    outputs = []
    for apply_slot_pos in range(slot_count):
        outputs.append(
            lax.cond(
                valid[apply_slot_pos],
                lambda values: apply_slot(left_prod[apply_slot_pos], apply_portion[apply_slot_pos]),
                lambda values: values,
                zeros_rows[apply_slot_pos],
            )
        )
    direction = jnp.stack(outputs)
    moment_one = 0.9 * first_moment + 0.1 * mine
    moment_two = 0.999 * second_moment + 0.001 * mine * mine
    adam = moment_one / (jnp.sqrt(moment_two) + 1e-08)
    adam_sq, dir_sq = lax.psum(
        (jnp.sum(adam * adam, axis=(1, 2)), jnp.sum(direction * direction, axis=(1, 2))),
        ("tensor", "section"),
    )
    graft = jnp.sqrt(adam_sq) / (jnp.sqrt(dir_sq) + 1e-06)
    mask = valid[:, None, None]
    new_left = jnp.where(mask, 0.5 * left_stat + 0.5 * left_gram, left_stat)
    new_right = jnp.where(mask, 0.5 * right_stat + 0.5 * right_gram, right_stat)
    new_first = jnp.where(mask, moment_one, first_moment)
    new_second = jnp.where(mask, moment_two, second_moment)
    my_weights = jnp.take(weights, picks, axis=0)
    new_rows = (my_weights.astype(jnp.float32) - 0.05 * graft[:, None, None] * direction).astype(
        jnp.bfloat16
    )
    slot_ids = jnp.arange(slot_block.shape[0], dtype=jnp.int32)
    holders = [
        jnp.sum(slot_ids * (slot_block == member).astype(jnp.int32))
        for member in range(block_count)
    ]
    published = []
    for member in range(block_count):
        owner = holders[member] // slot_count
        within = holders[member] % slot_count
        chosen = lax.dynamic_index_in_dim(new_rows, within, 0, keepdims=False)
        published.append(spread(chosen, "shard", owner))
    new_weights = jnp.stack(published)
    return (new_weights, new_left, new_right, new_first, new_second)


def solution(mesh):
    placed = (
        P(None, ("shard", "tensor", "section"), None),
        P(None, ("shard", "tensor", "section"), None),
        P(None, ("tensor", "section"), None),
        P(),
        P("shard", ("tensor", "section"), None),
        P("shard", ("tensor", "section"), None),
        P("shard", ("tensor", "section"), None),
        P("shard", ("tensor", "section"), None),
        P("shard", ("tensor", "section"), None),
        P("shard", ("tensor", "section"), None),
    )
    return jax.shard_map(
        on_device,
        mesh=mesh,
        in_specs=placed,
        out_specs=(
            P(None, ("tensor", "section"), None),
            P("shard", ("tensor", "section"), None),
            P("shard", ("tensor", "section"), None),
            P("shard", ("tensor", "section"), None),
            P("shard", ("tensor", "section"), None),
        ),
        check_vma=False,
    )
```

profile of v0, /device:TPU:0, one launch (start us, length us, event | category | flops | bytes accessed | tf_op | source)
XLA Modules:
  0.0 413.0 jit_solution(5907693126761822649)
XLA Ops:
  7.2 2.4 fusion.108
  9.6 2.1 fusion.111
  13.4 4.1 maximum_multiply_fusion
  17.5 9.7 %copy.20 = f32[768,3072]{1,0:T(8,128)} copy(f32[768,3072]{0,1:T(8,128)} %maximum_multiply_fusion) | data formatting | bytes 18874368
  27.2 114.2 %reduce-scatter.4.cloned.1.call-done = f32[48,3072]{1,0:T(8,128)} async-done(((f32[768,3072]{1,0:T(8,128)}), f32[48,3072]{1,0:T(8,128)}) %reduce-scatter.4.cloned.1.call-update) | async-done | bytes 589840
  144.4 29.8 %all-reduce.5.cloned.1.call-done = f32[48,4,768]{2,0,1:T(8,128)} async-done(((f32[48,4,768]{2,0,1:T(8,128)}), f32[48,4,768]{2,0,1:T(8,128)}) %all-reduce.5.cloned.1.call-update) | async-done | bytes 589840 | tf_op jit(solution)/shard_map/psum | solution.py:56
  192.7 66.0 %all-gather.5.cloned.1.call-done = f32[4,768,768]{2,1,0:T(8,128)} async-done(((f32[4,48,768]{2,1,0:T(8,128)}), f32[4,768,768]{2,1,0:T(8,128)}) %all-gather.5.cloned.1.call-update) | async-done | bytes 9437200 | tf_op jit(solution)/shard_map/all_gather | solution.py:67
  258.8 11.2 %conditional.10 = (f32[48,768]{1,0:T(8,128)S(1)}, f32[1,48,768]{2,1,0:T(8,128)S(1)}, f32[1,48,768]{2,1,0:T(8,128)S(1)}) conditional(s32[]{:T(128)} %bitcast.42, () %tuple.93, (f32[4,48,768]{2,1,0:T(8,128)}, f32[4,768,768]{2,1,0:T(8,128)}, f32[4,48,768]{2,1,0:T(8,128)}, s32[]{:T(128)}) %tuple.90), branch_computations={%region_9.10_spmd, %region_10.11_spmd} | conditional | flops 1019215872 | bytes 12927038 | solution.py:73
  259.0 1.8 slice.65
  262.5 3.3 fusion.31
  265.7 4.2 %fusion.33 = f32[1,48,768]{2,1,0:T(8,128)S(1)} fusion(f32[4,48,768]{2,1,0:T(8,128)} %get-tuple-element.80, f32[4,768,768]{2,1,0:T(8,128)} %get-tuple-element.79), kind=kOutput, calls=%fused_computation.29 | convolution fusion | flops 339738624 | bytes 2654208 | tf_op jit(solution)/shard_map/cond/branch_1_fun/dot_general | solution.py:16
  271.4 10.8 %conditional.14 = (f32[48,768]{1,0:T(8,128)S(1)}, f32[1,48,768]{2,1,0:T(8,128)S(1)}, f32[1,48,768]{2,1,0:T(8,128)S(1)}) conditional(s32[]{:T(128)} %bitcast.44, () %tuple.99, (f32[4,48,768]{2,1,0:T(8,128)}, f32[4,768,768]{2,1,0:T(8,128)}, f32[4,48,768]{2,1,0:T(8,128)}, s32[]{:T(128)}) %tuple.90), branch_computations={%region_17.18_spmd, %region_18.19_spmd} | conditional | flops 1019215872 | bytes 12927038 | solution.py:73
  271.4 1.8 slice.73
  275.0 3.3 fusion.85
  278.2 4.0 fusion.87
  282.3 58.2 %all-gather.3.cloned.1.call-done = f32[4,768,768]{2,1,0:T(8,128)} async-done(((f32[4,48,768]{2,1,0:T(8,128)}), f32[4,768,768]{2,1,0:T(8,128)}) %all-gather.3.cloned.1.call-update) | async-done | bytes 9437200 | tf_op jit(solution)/shard_map/all_gather | solution.py:87
  340.5 3.2 conditional.11
  340.5 3.2 fusion.51
  344.6 3.2 conditional.15
  344.6 3.2 fusion.105
  348.0 3.3 fusion.133
  351.3 30.8 %all-reduce = (f32[4]{0:T(128)S(1)}, f32[4]{0:T(128)S(1)}) all-reduce(f32[4]{0:T(128)S(1)} %multiply_reduce_fusion, f32[4]{0:T(128)S(1)} %get-tuple-element.140), channel_id=1, replica_groups=mesh['shard'=2,'tensor'=4,'section'=4] {'tensor','section'}, use_global_device_ids=true, to_apply=%region_22.23 | all-reduce | flops 8 | bytes 64 | tf_op jit(solution)/shard_map/psum | solution.py:102
  383.1 21.7 %all-reduce.7.cloned.1.call-done = (bf16[1,48,768]{2,1,0:T(8,128)(2,1)}, bf16[1,48,768]{2,1,0:T(8,128)(2,1)}, bf16[1,48,768]{2,1,0:T(8,128)(2,1)}, bf16[1,48,768]{2,1,0:T(8,128)(2,1)}) async-done(((bf16[1,48,768]{2,1,0:T(8,128)(2,1)}, bf16[1,48,768]{2,1,0:T(8,128)(2,1)}, bf16[1,48,768]{2,1,0:T(8,128)(2,1)}, bf16[1,48,768]{2,1,0:T(8,128)(2,1)}), (bf16[1,48,768]{2,1,0:T(8,128)(2,1)}, ...) | async-done | bytes 294928 | tf_op jit(solution)/shard_map/psum | solution.py:10
  404.7 1.7 pad_maximum_fusion.1
  (69 shorter events, 17.0 us)
Async XLA Ops:
  7.2 184.8 %copy-start = (bf16[4,48,768]{2,1,0:T(8,128)(2,1)S(1)}, bf16[4,48,768]{2,1,0:T(8,128)(2,1)}, u32[]{:S(2)}) copy-start(bf16[4,48,768]{2,1,0:T(8,128)(2,1)} %param.28) | copy-start | bytes 884740
  7.2 2.4 copy-start.3
  7.2 134.2 %reduce-scatter.4.cloned.1.call-start = ((), (), s32[]{:S(2)}) async-start(), calls=%async_computation.4 | async-start | bytes 10027008
  9.6 2.1 copy-start.4
  27.2 117.1 %copy-start.14 = (s32[8]{0:T(128)S(1)}, s32[8]{0:T(128)}, u32[]{:S(2)}) copy-start(s32[8]{0:T(128)} %param.29) | copy-start | bytes 100
  27.2 147.0 %all-reduce.5.cloned.1.call-start = ((), (), s32[]{:S(2)}) async-start(), calls=%async_computation.1 | async-start | bytes 1179648 | tf_op jit(solution)/shard_map/psum | solution.py:56
  142.9 32.9 %copy-start.5 = (f32[4,48,768]{2,1,0:T(8,128)S(1)}, f32[4,48,768]{2,1,0:T(8,128)}, u32[]{:S(2)}) copy-start(f32[4,48,768]{2,1,0:T(8,128)} %param.35) | copy-start | bytes 1769476
  144.2 114.5 %all-gather.5.cloned.1.call-start = ((), (), s32[]{:S(2)}) async-start(), calls=%async_computation.3 | async-start | bytes 10027008 | tf_op jit(solution)/shard_map/all_gather | solution.py:67
  177.1 163.4 %all-gather.3.cloned.1.call-start = ((), (), s32[]{:S(2)}) async-start(), calls=%async_computation.2 | async-start | bytes 10027008 | tf_op jit(solution)/shard_map/all_gather | solution.py:87
  177.7 227.1 %all-reduce.7.cloned.1.call-start = ((), (), s32[]{:S(2)}) async-start(), calls=%async_computation.5 | async-start | bytes 589824 | tf_op jit(solution)/shard_map/psum | solution.py:10
  270.0 0.7 copy-start.7
  270.7 0.7 copy-start.8
  270.7 0.7 copy-start.9
  282.3 61.4 %copy-start.10 = (f32[1,48,768]{2,1,0:T(8,128)}, f32[1,48,768]{2,1,0:T(8,128)S(1)}, u32[]{:S(2)}) copy-start(f32[1,48,768]{2,1,0:T(8,128)S(1)} %get-tuple-element.120) | copy-start | bytes 442372
  282.3 61.4 %copy-start.11 = (f32[1,48,768]{2,1,0:T(8,128)}, f32[1,48,768]{2,1,0:T(8,128)S(1)}, u32[]{:S(2)}) copy-start(f32[1,48,768]{2,1,0:T(8,128)S(1)} %get-tuple-element.124) | copy-start | bytes 442372
  282.3 61.4 %copy-start.12 = (f32[48,768]{1,0:T(8,128)}, f32[48,768]{1,0:T(8,128)S(1)}, u32[]{:S(2)}) copy-start(f32[48,768]{1,0:T(8,128)S(1)} %get-tuple-element.116) | copy-start | bytes 442372
  343.7 0.9 copy-start.13
  343.8 4.2 %copy-start.2 = (f32[4,48,768]{2,1,0:T(8,128)S(1)}, f32[4,48,768]{2,1,0:T(8,128)}, u32[]{:S(2)}) copy-start(f32[4,48,768]{2,1,0:T(8,128)} %get-tuple-element.136) | copy-start | bytes 1769476
  343.8 4.2 %copy-start.6 = (f32[4,48,768]{2,1,0:T(8,128)S(1)}, f32[4,48,768]{2,1,0:T(8,128)}, u32[]{:S(2)}) copy-start(f32[4,48,768]{2,1,0:T(8,128)} %param.34) | copy-start | bytes 1769476
  348.0 58.5 %copy-start.1 = (bf16[4,48,768]{2,1,0:T(8,128)(2,1)S(1)}, bf16[4,48,768]{2,1,0:T(8,128)(2,1)}, u32[]{:S(2)}) copy-start(bf16[4,48,768]{2,1,0:T(8,128)(2,1)} %param.28) | copy-start | bytes 884740
Sparse Core Ops, SparseCore 0:
  27.3 114.0 reduce-scatter.3
  144.4 29.7 all-reduce.4
  177.2 81.4 all-gather.4
  260.9 79.5 all-gather.2
  383.2 21.4 all-reduce.6
where the time goes:
time: 414 us; the launch traced here: 413 us
  waiting for transfers between devices  290 us (70%)
  blocking collectives  30.8 us (7%)
  matrix products  30.6 us (7%)
  between operations  27.2 us (7%)
  local copies, waits for them, and re-layouts  21.3 us (5%)
  other arithmetic  12.2 us (3%)
    unnamed x6, waiting for transfers between devices  115 us
    all_gather x1, waiting for transfers between devices, on_device(): portion = lax.all_gather(mine, ('tensor', 'section'), axis=1, tiled=True)  66 us
    all_gather x1, waiting for transfers between devices, on_device(): lax.all_gather(right_root, ('tensor', 'section'), axis=1, tiled=True)  58.2 us
    psum x1, blocking collectives, on_device(): lax.psum((jnp.sum(adam * adam, axis=(1, 2)), jnp.sum(direction * directio...  30.8 us
    psum x1, waiting for transfers between devices, on_device(): grad_rows = lax.psum(partial_rows, 'shard')  29.8 us
    psum x1, waiting for transfers between devices, spread(): return lax.psum(kept, axis)  21.7 us
    unnamed x32, local copies, waits for them, and re-layouts  13.4 us
    dot_general x2, matrix products, absorb_slot(): block_part = jnp.dot(mine_rows, portion.T, precision=highest)  8.3 us
  transfers between devices with their start and end apart: 5, of which 5 were waited for; matrix products, arithmetic and copies ran while one was open for 6% of the time, Pallas kernels for 0%

commit v1 on v0

--- a/solution.py
+++ b/solution.py
@@ -3,6 +3,23 @@
 import jax.numpy as jnp
 from jax import lax
 from jax.sharding import PartitionSpec as P
+
+
+def joined_along(blocks, dim):
+    shape = list(blocks.shape[1:])
+    shape[dim] *= blocks.shape[0]
+    return jnp.moveaxis(blocks, 0, dim).reshape(shape)
+
+
+def grow_blocks(x, axis):
+    length, position = (lax.axis_size(axis), lax.axis_index(axis))
+    tiles, distance = (x[None], 1)
+    while distance < length:
+        other = lax.ppermute(tiles, axis, [(i, i ^ distance) for i in range(length)])
+        low = position & distance == 0
+        tiles = jnp.concatenate([jnp.where(low, tiles, other), jnp.where(low, other, tiles)])
+        distance *= 2
+    return tiles
 
 
 def spread(value, axis, source):
@@ -64,7 +81,7 @@
     col_first = group_idx * row_count
     zeros_rows = jnp.zeros((slot_count, row_count, block_size), jnp.float32)
     totals = (zeros_rows, zeros_rows, zeros_rows)
-    portion = lax.all_gather(mine, ("tensor", "section"), axis=1, tiled=True)
+    portion = joined_along(grow_blocks(mine, ("tensor", "section")), 1)
     lefts = []
     rights = []
     prods = []

time: 414 us -> 634 us (1.53)
  waiting for transfers between devices: 290 us -> 478 us
  other arithmetic: 12.2 us -> 31.3 us
    ppermute x0 -> x4, waiting for transfers between devices: none -> 311 us  [grow_blocks(): lax.ppermute(tiles, axis, [(i, i ^ distance) for i in range(length)])]
    all_gather x1 -> x0, waiting for transfers between devices: 66 us -> none  [on_device(): portion = lax.all_gather(mine, ('tensor', 'section'), axis=1, tiled=True)]
    all_gather x1, waiting for transfers between devices: 58.2 us -> 0.02 us  [on_device(): lax.all_gather(right_root, ('tensor', 'section'), axis=1, tiled=True)]
    select_n x0 -> x4, other arithmetic: none -> 10.8 us  [grow_blocks(): jnp.where(low, tiles, other)]
    unnamed x32 -> x48, local copies, waits for them, and re-layouts: 13.4 us -> 14.7 us
    unnamed x6 -> x5, waiting for transfers between devices: 115 us -> 115 us
  transfers between devices with their start and end apart: 5 -> 8, of which waited for: 5 -> 7; matrix products, arithmetic and copies ran while one was open for 6% -> 8% of each run, Pallas kernels for 0% -> 0%
where the time goes in v1:
time: 634 us; the launch traced here: 633 us
  waiting for transfers between devices  478 us (75%)
  blocking collectives  32.2 us (5%)
  other arithmetic  31.3 us (5%)
  matrix products  30.5 us (5%)
  local copies, waits for them, and re-layouts  27.5 us (4%)
  between operations  27.1 us (4%)
    ppermute x4, waiting for transfers between devices, grow_blocks(): lax.ppermute(tiles, axis, [(i, i ^ distance) for i in range(length)])  311 us
    unnamed x5, waiting for transfers between devices  115 us
    psum x1, blocking collectives, on_device(): lax.psum((jnp.sum(adam * adam, axis=(1, 2)), jnp.sum(direction * directio...  32.2 us
    psum x1, waiting for transfers between devices, on_device(): grad_rows = lax.psum(partial_rows, 'shard')  29.1 us
    psum x1, waiting for transfers between devices, spread(): return lax.psum(kept, axis)  22.4 us
    unnamed x48, local copies, waits for them, and re-layouts  14.7 us
  transfers between devices with their start and end apart: 8, of which 7 were waited for; matrix products, arithmetic and copies ran while one was open for 8% of the time, Pallas kernels for 0%

profile of v1, /device:TPU:0, one launch (start us, length us, event | category | flops | bytes accessed | tf_op | source)
XLA Modules:
  0.0 632.7 jit_solution(13185630271887620476)
XLA Ops:
  13.4 4.0 maximum_multiply_fusion
  17.5 9.6 %copy.23 = f32[768,3072]{1,0:T(8,128)} copy(f32[768,3072]{0,1:T(8,128)} %maximum_multiply_fusion) | data formatting | bytes 18874368
  27.2 114.2 %reduce-scatter.4.cloned.1.call-done = f32[48,3072]{1,0:T(8,128)} async-done(((f32[768,3072]{1,0:T(8,128)}), f32[48,3072]{1,0:T(8,128)}) %reduce-scatter.4.cloned.1.call-update) | async-done | bytes 589840
  145.1 29.1 %all-reduce.5.cloned.1.call-done = f32[48,4,768]{2,0,1:T(8,128)} async-done(((f32[48,4,768]{2,0,1:T(8,128)}), f32[48,4,768]{2,0,1:T(8,128)}) %all-reduce.5.cloned.1.call-update) | async-done | bytes 589840 | tf_op jit(solution)/shard_map/psum | solution.py:73
  181.5 33.1 %collective-permute-done.1 = f32[2,4,48,768]{3,2,1,0:T(8,128)S(1)} collective-permute-done((f32[2,4,48,768]{3,2,1,0:T(8,128)}, f32[2,4,48,768]{3,2,1,0:T(8,128)S(1)}, u32[]{:S(2)}, u32[]{:S(2)}) %collective-permute-start.1) | collective-permute-done | bytes 1179680 | tf_op jit(solution)/shard_map/ppermute | solution.py:18
  217.8 88.5 %collective-permute-done.2 = f32[4,4,48,768]{3,2,1,0:T(8,128)} collective-permute-done((f32[4,4,48,768]{3,2,1,0:T(8,128)S(1)}, f32[4,4,48,768]{3,2,1,0:T(8,128)}, u32[]{:S(2)}, u32[]{:S(2)}) %collective-permute-start.2) | collective-permute-done | bytes 2359328 | tf_op jit(solution)/shard_map/ppermute | solution.py:18
  309.1 2.8 pad_maximum_fusion
  329.9 187.8 %collective-permute-done.3 = f32[8,4,48,768]{3,2,1,0:T(8,128)} collective-permute-done((f32[8,4,48,768]{3,2,1,0:T(8,128)}, f32[8,4,48,768]{3,2,1,0:T(8,128)}, u32[]{:S(2)}, u32[]{:S(2)}) %collective-permute-start.3) | collective-permute-done | bytes 4718624 | tf_op jit(solution)/shard_map/ppermute | solution.py:18
  517.8 7.6 %broadcast_select_fusion.1 = (f32[8,4,48,768]{3,2,1,0:T(8,128)}, f32[8,4,48,768]{3,2,1,0:T(8,128)}) fusion(f32[8,4,48,768]{3,2,1,0:T(8,128)} %collective-permute-done.3, pred[]{:T(512)S(6)} %eq.43, f32[4,4,48,768]{3,2,1,0:T(8,128)} %copy-done.2, f32[4,4,48,768]{3,2,1,0:T(8,128)S(1)} %get-tuple-element.141), kind=kLoop, calls=%fused_computation.91 | loop fusion | flops 3538944 | bytes 18874368 | tf_op jit(solution)/shard_map/jit(_where)/select_n | solution.py:20
  525.4 4.4 maximum_bitcast_fusion
  529.8 4.2 copy.20
  535.0 10.8 %conditional.10 = (f32[48,768]{1,0:T(8,128)S(1)}, f32[1,48,768]{2,1,0:T(8,128)S(1)}, f32[1,48,768]{2,1,0:T(8,128)S(1)}) conditional(s32[]{:T(128)} %bitcast.45, () %tuple.93, (f32[4,48,768]{2,1,0:T(8,128)}, f32[4,768,768]{2,1,0:T(8,128)}, f32[4,48,768]{2,1,0:T(8,128)}, s32[]{:T(128)}) %tuple.151), branch_computations={%region_9.10_spmd, %region_10.11_spmd} | conditional | flops 1019215872 | bytes 12927038 | solution.py:90
  538.5 3.3 fusion.31
  541.8 4.0 fusion.33
  547.5 10.8 %conditional.14 = (f32[48,768]{1,0:T(8,128)S(1)}, f32[1,48,768]{2,1,0:T(8,128)S(1)}, f32[1,48,768]{2,1,0:T(8,128)S(1)}) conditional(s32[]{:T(128)} %bitcast.47, () %tuple.99, (f32[4,48,768]{2,1,0:T(8,128)}, f32[4,768,768]{2,1,0:T(8,128)}, f32[4,48,768]{2,1,0:T(8,128)}, s32[]{:T(128)}) %tuple.153), branch_computations={%region_17.18_spmd, %region_18.19_spmd} | conditional | flops 1019215872 | bytes 12927038 | solution.py:90
  551.0 3.3 fusion.85
  554.3 4.0 fusion.87
  558.4 3.2 conditional.11
  558.4 3.2 fusion.51
  562.0 3.3 conditional.15
  562.1 3.3 fusion.105
  565.6 3.3 fusion.133
  568.9 32.2 %all-reduce = (f32[4]{0:T(128)S(1)}, f32[4]{0:T(128)S(1)}) all-reduce(f32[4]{0:T(128)S(1)} %multiply_reduce_fusion, f32[4]{0:T(128)S(1)} %get-tuple-element.146), channel_id=1, replica_groups=mesh['shard'=2,'tensor'=4,'section'=4] {'tensor','section'}, use_global_device_ids=true, to_apply=%region_22.23 | all-reduce | flops 8 | bytes 64 | tf_op jit(solution)/shard_map/psum | solution.py:119
  602.0 22.4 %all-reduce.7.cloned.1.call-done = (bf16[1,48,768]{2,1,0:T(8,128)(2,1)}, bf16[1,48,768]{2,1,0:T(8,128)(2,1)}, bf16[1,48,768]{2,1,0:T(8,128)(2,1)}, bf16[1,48,768]{2,1,0:T(8,128)(2,1)}) async-done(((bf16[1,48,768]{2,1,0:T(8,128)(2,1)}, bf16[1,48,768]{2,1,0:T(8,128)(2,1)}, bf16[1,48,768]{2,1,0:T(8,128)(2,1)}, bf16[1,48,768]{2,1,0:T(8,128)(2,1)}), (bf16[1,48,768]{2,1,0:T(8,128)(2,1)}, ...) | async-done | bytes 294928 | tf_op jit(solution)/shard_map/psum | solution.py:27
  (99 shorter events, 41.2 us)
Async XLA Ops:
  7.2 321.5 %copy-start = (bf16[4,48,768]{2,1,0:T(8,128)(2,1)S(1)}, bf16[4,48,768]{2,1,0:T(8,128)(2,1)}, u32[]{:S(2)}) copy-start(bf16[4,48,768]{2,1,0:T(8,128)(2,1)} %param.28) | copy-start | bytes 884740
  7.2 2.4 copy-start.7
  7.2 134.2 %reduce-scatter.4.cloned.1.call-start = ((), (), s32[]{:S(2)}) async-start(), calls=%async_computation.3 | async-start | bytes 10027008
  9.6 2.1 copy-start.8
  27.1 117.9 %copy-start.22 = (s32[8]{0:T(128)S(1)}, s32[8]{0:T(128)}, u32[]{:S(2)}) copy-start(s32[8]{0:T(128)} %param.29) | copy-start | bytes 100
  27.1 147.0 %all-reduce.5.cloned.1.call-start = ((), (), s32[]{:S(2)}) async-start(), calls=%async_computation.1 | async-start | bytes 1179648 | tf_op jit(solution)/shard_map/psum | solution.py:73
  142.9 32.9 %copy-start.9 = (f32[4,48,768]{2,1,0:T(8,128)S(1)}, f32[4,48,768]{2,1,0:T(8,128)}, u32[]{:S(2)}) copy-start(f32[4,48,768]{2,1,0:T(8,128)} %param.35) | copy-start | bytes 1769476
  144.2 414.2 %all-gather.2.cloned.1.call-start = ((), (), s32[]{:S(2)}) async-start(), calls=%async_computation.2 | async-start | bytes 10027008 | tf_op jit(solution)/shard_map/all_gather | solution.py:104
  144.9 479.5 %all-reduce.7.cloned.1.call-start = ((), (), s32[]{:S(2)}) async-start(), calls=%async_computation.4 | async-start | bytes 589824 | tf_op jit(solution)/shard_map/psum | solution.py:27
  176.8 3.2 copy-start.5
  176.8 2.0 collective-permute-start
  180.0 34.5 %collective-permute-start.1 = (f32[2,4,48,768]{3,2,1,0:T(8,128)}, f32[2,4,48,768]{3,2,1,0:T(8,128)S(1)}, u32[]{:S(2)}, u32[]{:S(2)}) collective-permute-start(f32[2,4,48,768]{3,2,1,0:T(8,128)} %pad_maximum_fusion.2), channel_id=1, source_target_pairs={{0,2},{1,3},{2,0},{3,1},{4,6},{5,7},{6,4},{7,5},{8,10},{9,11},{10,... | collective-permute-start | bytes 3538952 | tf_op jit(solution)/shard_map/ppermute | solution.py:18
  214.8 1.6 copy-start.4
  216.4 89.9 %collective-permute-start.2 = (f32[4,4,48,768]{3,2,1,0:T(8,128)S(1)}, f32[4,4,48,768]{3,2,1,0:T(8,128)}, u32[]{:S(2)}, u32[]{:S(2)}) collective-permute-start(f32[4,4,48,768]{3,2,1,0:T(8,128)S(1)} %pad_maximum_fusion.1), channel_id=1, source_target_pairs={{0,4},{1,5},{2,6},{3,7},{4,0},{5,1},{6,2},{7,3},{8,12},{9,13},{10,... | collective-permute-start | bytes 7077896 | tf_op jit(solution)/shard_map/ppermute | solution.py:18
  309.1 2.9 copy-start.2
  312.0 205.8 %collective-permute-start.3 = (f32[8,4,48,768]{3,2,1,0:T(8,128)}, f32[8,4,48,768]{3,2,1,0:T(8,128)}, u32[]{:S(2)}, u32[]{:S(2)}) collective-permute-start(f32[8,4,48,768]{3,2,1,0:T(8,128)} %pad_maximum_fusion), channel_id=1, source_target_pairs={{0,8},{1,9},{2,10},{3,11},{4,12},{5,13},{6,14},{7,15},{8,0},{9,1},... | collective-permute-start | bytes 14155784 | tf_op jit(solution)/shard_map/ppermute | solution.py:18
  558.3 3.3 copy-start.20
  558.3 3.3 copy-start.21
  562.0 3.5 copy-start.6
  562.0 3.5 copy-start.10
  562.0 3.5 copy-start.12
  562.0 3.5 copy-start.13
  565.5 35.5 %copy-start.11 = (bf16[4,48,768]{2,1,0:T(8,128)(2,1)S(1)}, bf16[4,48,768]{2,1,0:T(8,128)(2,1)}, u32[]{:S(2)}) copy-start(bf16[4,48,768]{2,1,0:T(8,128)(2,1)} %gather_fusion) | copy-start | bytes 884740
  565.6 60.6 %copy-start.1 = (bf16[4,48,768]{2,1,0:T(8,128)(2,1)S(1)}, bf16[4,48,768]{2,1,0:T(8,128)(2,1)}, u32[]{:S(2)}) copy-start(bf16[4,48,768]{2,1,0:T(8,128)(2,1)} %param.28) | copy-start | bytes 884740
  (7 other events, 5.1 us)
Sparse Core Ops, SparseCore 0:
  27.2 114.0 reduce-scatter.3
  144.3 29.7 all-reduce.4
  176.4 112.9 all-gather.1
  602.1 22.2 all-reduce.6
